TPU v7x, 128 devices: a whole 4x4x4 slice. The times are simulated.
128 devices in a mesh: tm: 16 (over x, y_lo, core), space: 8 (over z, y_hi).
Axes of the slice: x: 4, y: 4 (y_hi: 2, y_lo: 2; y = y_hi * 2 + y_lo), z: 4, core: 2. Of those that a mesh axis runs over, the one named last changes fastest.
Arguments:
- input_field: float32 [64, 32, 32, 1024], P('tm', None, 'space'), may hold values from -6 to 6
- cotangent: float32 [64, 32, 32, 1024], P('tm', None, 'space'), may hold values from -6 to 6
- spectral_weights: float32 [2, 2, 16, 32, 32], replicated, may hold values from -0.75 to 0.75
- conv_kernel: float32 [2, 3, 32, 32], replicated, may hold values from -0.625 to 0.625
- mode_list: int32 [16], replicated, may hold values from 0 to 31, as said below
Outputs:
- grad_input: float32 [64, 32, 32, 1024], P('tm', None, 'space')
- grad_spectral: float32 [2, 2, 16, 32, 32], P(None, None, 'tm')
- grad_kernel: float32 [2, 3, 32, 32], replicated
Inputs may be any that keep to these rules, and one draw needn't show every extreme that they name: `mode_list`: 16 distinct frequencies in ascending order, with 0 and 31 among them.
All inputs are finite; a program needn't handle non-finite values.
Results may differ from a plain program's by a relative error of at most 0.00014.
Values sent between devices are 32-bit elements; how exact they have to be, the bound alone decides.
No kernel may reach another device: no remote copies, remote signals or barrier semaphores. Data moves between devices by JAX's collectives and lax.ppermute only.
A program may use at most 128 MiB of HBM per device.

v0:
```python
import math
import jax
import jax.numpy as jnp
from jax import lax
from jax.sharding import PartitionSpec as P

HIGHEST = lax.Precision.HIGHEST


def extended(value, sides, width):
    for axis, dim in sides:
        size, length = (lax.axis_size(axis), value.shape[dim])
        up = [(i, (i + 1) % size) for i in range(size - 1)]
        down = [(j, i) for i, j in up]
        last = lax.slice_in_dim(value, length - width, length, axis=dim)
        initial = lax.slice_in_dim(value, 0, width, axis=dim)
        before = lax.ppermute(last, axis, up)
        after = lax.ppermute(initial, axis, down)
        value = jnp.concatenate([before, value, after], axis=dim)
    return value


def tables(mode_list, time_count, total_time):
    time_steps = jnp.arange(time_count, dtype=jnp.int32)
    phase_index = mode_list[:, None] * time_steps[None, :] % total_time
    angles = phase_index.astype(jnp.float32) * (2.0 * math.pi / total_time)
    return (jnp.cos(angles), jnp.sin(angles))


def forward_dft(cosine_table, sine_table, flattened):
    time_count = flattened.shape[0]
    rows = flattened.reshape(time_count, -1)
    cosine_part = jnp.dot(cosine_table, rows, precision=HIGHEST)
    sine_part = -jnp.dot(sine_table, rows, precision=HIGHEST)
    stacked = jnp.stack([cosine_part, sine_part], axis=1)
    return stacked.reshape(cosine_table.shape[0], 2, flattened.shape[1], flattened.shape[2])


def inverse_dft(cosine_table, sine_table, coefficients, factor):
    mode_count = coefficients.shape[0]
    cosine_term = jnp.dot(
        cosine_table.T, coefficients[:, 0].reshape(mode_count, -1), precision=HIGHEST
    )
    sine_term = jnp.dot(sine_table.T, coefficients[:, 1].reshape(mode_count, -1), precision=HIGHEST)
    result = factor * (cosine_term - sine_term)
    return result.reshape(cosine_table.shape[1], coefficients.shape[2], coefficients.shape[3])


def mode_product(values, weight):
    return jnp.einsum("mcn,mcd->mdn", values, weight, precision=HIGHEST)


def mode_adjoint(values, weight):
    return jnp.einsum("mdn,mcd->mcn", values, weight, precision=HIGHEST)


def mode_outer(left_values, right_values):
    return jnp.einsum("mcn,mdn->mcd", left_values, right_values, precision=HIGHEST)


def channel_mix(coefficients, weight):
    real_part = mode_product(coefficients[:, 0], weight[0]) - mode_product(
        coefficients[:, 1], weight[1]
    )
    imag_part = mode_product(coefficients[:, 1], weight[0]) + mode_product(
        coefficients[:, 0], weight[1]
    )
    return jnp.stack([real_part, imag_part], axis=1)


def channel_mix_adjoint(sens_modes, weight):
    real_part = mode_adjoint(sens_modes[:, 0], weight[0]) + mode_adjoint(
        sens_modes[:, 1], weight[1]
    )
    imag_part = mode_adjoint(sens_modes[:, 1], weight[0]) - mode_adjoint(
        sens_modes[:, 0], weight[1]
    )
    return jnp.stack([real_part, imag_part], axis=1)


def weight_grad(coefficients, sens_modes):
    real_part = mode_outer(coefficients[:, 0], sens_modes[:, 0]) + mode_outer(
        coefficients[:, 1], sens_modes[:, 1]
    )
    imag_part = mode_outer(coefficients[:, 0], sens_modes[:, 1]) - mode_outer(
        coefficients[:, 1], sens_modes[:, 0]
    )
    return jnp.stack([real_part, imag_part], axis=0)


def convolve(padded, kernel, cells_x):
    result = jnp.einsum("tcxs,cd->tdxs", padded[:, :, 0:cells_x], kernel[0], precision=HIGHEST)
    for offset in range(1, 3):
        result = result + jnp.einsum(
            "tcxs,cd->tdxs",
            padded[:, :, offset : offset + cells_x],
            kernel[offset],
            precision=HIGHEST,
        )
    return result


def convolve_adjoint(sens_padded, kernel, cells_x):
    result = jnp.einsum(
        "tdxs,cd->tcxs", sens_padded[:, :, 2 : 2 + cells_x], kernel[0], precision=HIGHEST
    )
    for offset in range(1, 3):
        result = result + jnp.einsum(
            "tdxs,cd->tcxs",
            sens_padded[:, :, 2 - offset : 2 - offset + cells_x],
            kernel[offset],
            precision=HIGHEST,
        )
    return result


def gelu_exact(values):
    return jax.nn.gelu(values, approximate=False)


def on_device(input_field, cotangent, spectral_weights, conv_kernel, mode_list):
    groups = lax.axis_size("tm")
    total_time = input_field.shape[0] * groups
    layers = conv_kernel.shape[0]
    factor = 2.0 / total_time
    cosine_all, sine_all = tables(mode_list, total_time, total_time)
    state_field, gradient = (input_field, cotangent)
    time_local, channels, cells_x, cells_s = state_field.shape
    cell_count = cells_x * cells_s
    saved = []
    for layer_number in range(layers):
        padded = extended(state_field, (("space", 2),), 1)
        convolved = convolve(padded, conv_kernel[layer_number], cells_x)
        flattened = state_field.reshape(time_local, channels, cell_count)
        series_field = lax.all_to_all(flattened, "tm", split_axis=2, concat_axis=0, tiled=True)
        coefficients = forward_dft(cosine_all, sine_all, series_field)
        mixed = channel_mix(coefficients, spectral_weights[layer_number])
        returned = inverse_dft(cosine_all, sine_all, mixed, factor)
        spectral_part = lax.all_to_all(returned, "tm", split_axis=0, concat_axis=2, tiled=True)
        preact = spectral_part.reshape(state_field.shape) + convolved
        saved.append((padded, coefficients, preact))
        state_field = gelu_exact(preact)
    kernel_pieces = []
    mode_pieces = []
    for layer_number in reversed(range(layers)):
        padded, coefficients, preact = saved[layer_number]
        pullback = jax.vjp(gelu_exact, preact)[1]
        sensitivity = pullback(gradient)[0]
        kernel_piece = jnp.stack(
            [
                jnp.einsum(
                    "tcxs,tdxs->cd",
                    padded[:, :, offset : offset + cells_x],
                    sensitivity,
                    precision=HIGHEST,
                )
                for offset in range(3)
            ]
        )
        sens_padded = extended(sensitivity, (("space", 2),), 1)
        back_conv = convolve_adjoint(sens_padded, conv_kernel[layer_number], cells_x)
        flat_sens = sensitivity.reshape(time_local, channels, cell_count)
        series_sens = lax.all_to_all(flat_sens, "tm", split_axis=2, concat_axis=0, tiled=True)
        sens_modes = factor * forward_dft(cosine_all, sine_all, series_sens)
        mode_piece = weight_grad(coefficients, sens_modes)
        adjoint = channel_mix_adjoint(sens_modes, spectral_weights[layer_number])
        returned = inverse_dft(cosine_all, sine_all, adjoint, 1.0)
        back_spec = lax.all_to_all(returned, "tm", split_axis=0, concat_axis=2, tiled=True)
        gradient = back_spec.reshape(sensitivity.shape) + back_conv
        kernel_pieces.append(kernel_piece)
        mode_pieces.append(mode_piece)
    kernel_total = lax.psum(jnp.stack(kernel_pieces[::-1]), ("tm", "space"))
    mode_stack = lax.psum_scatter(
        jnp.stack(mode_pieces[::-1]), "tm", scatter_dimension=2, tiled=True
    )
    mode_total = lax.psum(mode_stack, "space")
    return (gradient, mode_total, kernel_total)


def solution(mesh):
    placed = (P("tm", None, "space", None), P("tm", None, "space", None), P(), P(), P())
    return jax.shard_map(
        on_device,
        mesh=mesh,
        in_specs=placed,
        out_specs=(P("tm", None, "space", None), P(None, None, "tm", None, None), P()),
        check_vma=False,
    )
```

profile of v0, /device:TPU:0, one launch (start us, length us, event | category | flops | bytes accessed | tf_op | source)
XLA Modules:
  0.0 852.2 jit_solution(5890445966441035744)
XLA Ops:
  14.9 8.5 reshape.161
  23.4 33.1 %all_to_all.120 = f32[16,1,32768]{2,1,0:T(1,128)} all-to-all(f32[16,1,32768]{2,1,0:T(1,128)S(1)} %reshape.161), channel_id=1, replica_groups=mesh['tm'=16,'space'=8] {'tm'}, dimensions={0} | all-to-all | bytes 4194304 | tf_op jit(solution)/shard_map/all_to_all | solution.py:135
  108.9 23.0 %collective-permute-done = f32[4,32,1,1024]{3,1,2,0:T(8,128)S(1)} collective-permute-done((f32[4,32,1,1024]{3,1,2,0:T(8,128)S(1)}, f32[4,32,1,1024]{3,1,2,0:T(8,128)S(1)}, u32[]{:S(2)}, u32[]{:S(2)}) %collective-permute-start) | collective-permute-done | bytes 524320 | tf_op jit(solution)/shard_map/ppermute | solution.py:17
  134.9 11.6 %collective-permute-done.1 = f32[4,32,1,1024]{3,1,2,0:T(8,128)S(1)} collective-permute-done((f32[4,32,1,1024]{3,1,2,0:T(8,128)S(1)}, f32[4,32,1,1024]{3,1,2,0:T(8,128)S(1)}, u32[]{:S(2)}, u32[]{:S(2)}) %collective-permute-start.1) | collective-permute-done | bytes 524320 | tf_op jit(solution)/shard_map/ppermute | solution.py:18
  155.9 10.0 %multiply_multiply_fusion.10 = (f32[4,32,4,1024]{3,1,2,0:T(8,128)S(1)}, f32[4,32,4,1024]{3,1,2,0:T(8,128)}) fusion(f32[4,32,5,1024]{3,1,2,0:T(8,128)} %constant_dynamic-update-slice_fusion.2, f32[2,3,32,32]{3,2,1,0:T(8,128)S(1)} %copy-done.28, f32[32,4,4,1024]{3,0,2,1:T(8,128)} %fusion.154, f32[4,4,1024,32]{2,3,1,0:T(8,128)} %fusion.157, ...), kind=kOutput, calls=%fused_computation.86 | convolution fusion | flops 236453888 | bytes 13123584 | tf_op jit(solution)/shard_map/tcxs,cd->tdxs/dot_general | solution.py:94
  171.8 9.5 %reshape.163 = f32[16,1,32768]{2,1,0:T(1,128)} reshape(f32[4096,4,32]{2,1,0:T(4,128)} %bitcast.414) | data formatting | bytes 4194304
  181.3 32.7 %all_to_all.121 = f32[16,1,32768]{2,1,0:T(1,128)} all-to-all(f32[16,1,32768]{2,1,0:T(1,128)} %reshape.163), channel_id=1, replica_groups=mesh['tm'=16,'space'=8] {'tm'}, dimensions={0} | all-to-all | bytes 4194304 | tf_op jit(solution)/shard_map/all_to_all | solution.py:135
  214.0 8.6 %reduce.1 = f32[16,32768]{1,0:T(8,128)} reduce(f32[16,1,32768]{2,1,0:T(1,128)} %all_to_all.121, f32[]{:T(128)} %broadcast.353), dimensions={1}, to_apply=%all_to_all.94.reduce_sub_computation | reduce | bytes 4194308 | tf_op jit(solution)/shard_map/all_to_all | solution.py:135
  230.3 8.4 copy.239
  270.5 23.8 %collective-permute-done.2 = f32[4,32,1,1024]{3,1,2,0:T(8,128)S(1)} collective-permute-done((f32[4,32,1,1024]{3,1,2,0:T(8,128)S(1)}, f32[4,32,1,1024]{3,1,2,0:T(8,128)S(1)}, u32[]{:S(2)}, u32[]{:S(2)}) %collective-permute-start.2) | collective-permute-done | bytes 524320 | tf_op jit(solution)/shard_map/ppermute | solution.py:17
  309.3 10.8 %fusion.26 = f32[4,32,4,1024]{3,1,2,0:T(8,128)} fusion(f32[4,32,4,1024]{3,2,1,0:T(4,128)} %param.6, f32[4,4,1024,32]{2,3,1,0:T(8,128)} %fusion.20, f32[4,4,1024,32]{2,3,1,0:T(8,128)} %fusion.142, f32[4,32,4,1024]{3,2,1,0:T(4,128)} %reshape.128, f32[4,32,1,1024]{3,1,2,0:T(8,128)} %collective-permute-done.3, f32[4,32,4,1024]{3,1,2,0:T(8,128)S(1)} %get-tuple-element.29, ...), kind=kOutput, calls=%fused_computation.38 | convolution fusion | flops 240779264 | bytes 13123584 | tf_op jit(solution)/shard_map/tcxs,cd->tdxs/dot_general | solution.py:94
  320.1 7.8 copy.332
  328.0 9.5 %reshape.165 = f32[16,1,32768]{2,1,0:T(1,128)} reshape(f32[4096,4,32]{2,1,0:T(4,128)} %bitcast.415) | data formatting | bytes 4194304
  337.5 32.9 %all_to_all.122 = f32[16,1,32768]{2,1,0:T(1,128)} all-to-all(f32[16,1,32768]{2,1,0:T(1,128)} %reshape.165), channel_id=1, replica_groups=mesh['tm'=16,'space'=8] {'tm'}, dimensions={0} | all-to-all | bytes 4194304 | tf_op jit(solution)/shard_map/all_to_all | solution.py:163
  370.4 8.6 %reduce.2 = f32[16,32768]{1,0:T(8,128)} reduce(f32[16,1,32768]{2,1,0:T(1,128)} %all_to_all.122, f32[]{:T(128)} %broadcast.353), dimensions={1}, to_apply=%all_to_all.100.reduce_sub_computation | reduce | bytes 4194308 | tf_op jit(solution)/shard_map/all_to_all | solution.py:163
  386.7 8.4 copy.254
  438.2 17.2 %collective-permute-done.4 = f32[4,32,1,1024]{3,1,2,0:T(8,128)S(1)} collective-permute-done((f32[4,32,1,1024]{3,1,2,0:T(8,128)S(1)}, f32[4,32,1,1024]{3,1,2,0:T(8,128)S(1)}, u32[]{:S(2)}, u32[]{:S(2)}) %collective-permute-start.4) | collective-permute-done | bytes 524320 | tf_op jit(solution)/shard_map/ppermute | solution.py:18
  464.0 9.6 %multiply_add_fusion = f32[4,32,4,1024]{3,1,2,0:T(8,128)S(1)} fusion(f32[4,32,4,1024]{3,2,1,0:T(4,128)} %reshape.133, f32[4,4,1024,32]{2,3,1,0:T(8,128)} %fusion.2, f32[4,4,1024,32]{2,3,1,0:T(8,128)} %fusion.140, f32[4,32,4,1024]{3,1,2,0:T(8,128)} %get-tuple-element.30, f32[4,32,4,1024]{3,1,2,0:T(8,128)} %fusion.26, ...), kind=kOutput, calls=%fused_computation.57 | convolution fusion | flops 240779264 | bytes 13123584 | tf_op jit(solution)/shard_map/tdxs,cd->tcxs/dot_general | solution.py:108
  479.6 9.5 %reshape.167 = f32[16,1,32768]{2,1,0:T(1,128)} reshape(f32[4096,4,32]{2,1,0:T(4,128)} %bitcast.416) | data formatting | bytes 4194304
  522.0 8.6 %reduce.3 = f32[16,32768]{1,0:T(8,128)} reduce(f32[16,1,32768]{2,1,0:T(1,128)} %all-to-all-done.6, f32[]{:T(128)} %broadcast.353), dimensions={1}, to_apply=%all_to_all.106.reduce_sub_computation | reduce | bytes 4194308 | tf_op jit(solution)/shard_map/all_to_all | solution.py:163
  538.3 8.1 copy.272
  569.6 88.0 %psum.15 = f32[2,3,32,32]{3,2,1,0:T(8,128)} all-reduce(f32[2,3,32,32]{3,2,1,0:T(8,128)S(1)} %pad_maximum_fusion.11), channel_id=1, replica_groups=mesh['tm'=16,'space'=8] {'tm','space'}, use_global_device_ids=true, to_apply=%region_2.3 | all-reduce | flops 6144 | bytes 49152 | tf_op jit(solution)/shard_map/psum | solution.py:172
  671.1 112.7 %all-reduce.3.cloned.1.call-done = f32[2,2,16,32,32]{4,3,2,1,0:T(8,128)} async-done(((f32[2,2,16,32,32]{4,3,2,1,0:T(8,128)}), f32[2,2,16,32,32]{4,3,2,1,0:T(8,128)}) %all-reduce.3.cloned.1.call-update) | async-done | bytes 262160
  785.1 43.4 %psum.14 = f32[2,2,1,32,32]{4,3,2,1,0:T(8,128)} all-reduce(f32[2,2,1,32,32]{4,3,2,1,0:T(8,128)S(1)} %constant_dynamic-slice_fusion), channel_id=1, replica_groups=mesh['tm'=16,'space'=8] {'space'}, use_global_device_ids=true, to_apply=%region_1.2 | all-reduce | flops 4096 | bytes 32768 | tf_op jit(solution)/shard_map/psum | solution.py:176
  (206 shorter events, 292.1 us)
Async XLA Ops:
  81.2 5.9 copy-start.11
  92.8 58.0 %all-to-all-start.1 = ((f32[64,32,256]{2,1,0:T(8,128)}), f32[64,32,256]{2,1,0:T(8,128)}, u32[]{:S(2)}, u32[]{:S(2)}) async-start(f32[64,32,256]{2,1,0:T(8,128)} %bitcast.439), calls=%async_computation.1 | async-start | bytes 4194304 | tf_op jit(solution)/shard_map/all_to_all | solution.py:139
  97.4 7.2 copy-start.28
  98.3 33.6 %collective-permute-start = (f32[4,32,1,1024]{3,1,2,0:T(8,128)S(1)}, f32[4,32,1,1024]{3,1,2,0:T(8,128)S(1)}, u32[]{:S(2)}, u32[]{:S(2)}) collective-permute-start(f32[4,32,1,1024]{3,1,2,0:T(8,128)S(1)} %copy.463), channel_id=1, source_target_pairs={{0,1},{1,2},{2,3},{3,4},{4,5},{5,6},{6,7},{8,9},{9,10},{10,11},{11... | collective-permute-start | bytes 1572872 | tf_op jit(solution)/shard_map/ppermute | solution.py:17
  103.2 43.2 %collective-permute-start.1 = (f32[4,32,1,1024]{3,1,2,0:T(8,128)S(1)}, f32[4,32,1,1024]{3,1,2,0:T(8,128)S(1)}, u32[]{:S(2)}, u32[]{:S(2)}) collective-permute-start(f32[4,32,1,1024]{3,1,2,0:T(8,128)S(1)} %copy.464), channel_id=1, source_target_pairs={{1,0},{2,1},{3,2},{4,3},{5,4},{6,5},{7,6},{9,8},{10,9},{11,10},{12... | collective-permute-start | bytes 1572872 | tf_op jit(solution)/shard_map/ppermute | solution.py:18
  134.9 12.5 %copy-start.23 = (f32[4,32,5,1024]{3,1,2,0:T(8,128)}, f32[4,32,5,1024]{3,1,2,0:T(8,128)S(1)}, u32[]{:S(2)}) copy-start(f32[4,32,5,1024]{3,1,2,0:T(8,128)S(1)} %get-tuple-element.24) | copy-start | bytes 7864324
  242.7 7.1 copy-start.13
  255.3 43.1 %all-to-all-start.3 = ((f32[64,32,256]{2,1,0:T(8,128)}), f32[64,32,256]{2,1,0:T(8,128)}, u32[]{:S(2)}, u32[]{:S(2)}) async-start(f32[64,32,256]{2,1,0:T(8,128)} %bitcast.440), calls=%async_computation.3 | async-start | bytes 4194304 | tf_op jit(solution)/shard_map/all_to_all | solution.py:139
  260.7 33.6 %collective-permute-start.2 = (f32[4,32,1,1024]{3,1,2,0:T(8,128)S(1)}, f32[4,32,1,1024]{3,1,2,0:T(8,128)S(1)}, u32[]{:S(2)}, u32[]{:S(2)}) collective-permute-start(f32[4,32,1,1024]{3,1,2,0:T(8,128)S(1)} %get-tuple-element.20), channel_id=1, source_target_pairs={{0,1},{1,2},{2,3},{3,4},{4,5},{5,6},{6,7},{8,9},{9,10},{10,11},{11... | collective-permute-start | bytes 1572872 | tf_op jit(solution)/shard_map/ppermute | solution.py:17
  265.8 43.5 %collective-permute-start.3 = (f32[4,32,1,1024]{3,1,2,0:T(8,128)}, f32[4,32,1,1024]{3,1,2,0:T(8,128)}, u32[]{:S(2)}, u32[]{:S(2)}) collective-permute-start(f32[4,32,1,1024]{3,1,2,0:T(8,128)} %get-tuple-element.19), channel_id=1, source_target_pairs={{1,0},{2,1},{3,2},{4,3},{5,4},{6,5},{7,6},{9,8},{10,9},{11,10},{12... | collective-permute-start | bytes 1572872 | tf_op jit(solution)/shard_map/ppermute | solution.py:18
  412.7 46.2 %all-to-all-start.5 = ((f32[64,32,256]{2,1,0:T(8,128)}), f32[64,32,256]{2,1,0:T(8,128)}, u32[]{:S(2)}, u32[]{:S(2)}) async-start(f32[64,32,256]{2,1,0:T(8,128)} %bitcast.438), calls=%async_computation.5 | async-start | bytes 4194304 | tf_op jit(solution)/shard_map/all_to_all | solution.py:168
  417.3 10.9 %copy-start = (f32[4,32,4,1024]{3,1,2,0:T(8,128)S(1)}, f32[4,32,4,1024]{3,1,2,0:T(8,128)}, u32[]{:S(2)}) copy-start(f32[4,32,4,1024]{3,1,2,0:T(8,128)} %fusion.26) | copy-start | bytes 6291460
  420.1 35.4 %collective-permute-start.4 = (f32[4,32,1,1024]{3,1,2,0:T(8,128)S(1)}, f32[4,32,1,1024]{3,1,2,0:T(8,128)S(1)}, u32[]{:S(2)}, u32[]{:S(2)}) collective-permute-start(f32[4,32,1,1024]{3,1,2,0:T(8,128)S(1)} %get-tuple-element.18), channel_id=1, source_target_pairs={{1,0},{2,1},{3,2},{4,3},{5,4},{6,5},{7,6},{9,8},{10,9},{11,10},{12... | collective-permute-start | bytes 1572872 | tf_op jit(solution)/shard_map/ppermute | solution.py:18
  421.4 42.6 %collective-permute-start.5 = (f32[4,32,1,1024]{3,1,2,0:T(8,128)}, f32[4,32,1,1024]{3,1,2,0:T(8,128)}, u32[]{:S(2)}, u32[]{:S(2)}) collective-permute-start(f32[4,32,1,1024]{3,1,2,0:T(8,128)} %get-tuple-element.17), channel_id=1, source_target_pairs={{0,1},{1,2},{2,3},{3,4},{4,5},{5,6},{6,7},{8,9},{9,10},{10,11},{11... | collective-permute-start | bytes 1572872 | tf_op jit(solution)/shard_map/ppermute | solution.py:17
  489.0 33.0 %all-to-all-start.6 = ((f32[16,1,32768]{2,1,0:T(1,128)}), f32[16,1,32768]{2,1,0:T(1,128)}, u32[]{:S(2)}, u32[]{:S(2)}) async-start(f32[16,1,32768]{2,1,0:T(1,128)} %reshape.167), calls=%async_computation.6 | async-start | bytes 4194304 | tf_op jit(solution)/shard_map/all_to_all | solution.py:163
  494.2 5.8 copy-start.10
  494.2 5.8 copy-start.16
  500.1 11.2 %copy-start.2 = (f32[4,32,4,1024]{3,2,1,0:T(4,128)S(1)}, f32[4,32,4,1024]{3,2,1,0:T(4,128)}, u32[]{:S(2)}) copy-start(f32[4,32,4,1024]{3,2,1,0:T(4,128)} %param.5) | copy-start | bytes 6291460
  502.7 163.9 %collective-permute-start.6 = (f32[4,32,1,1024]{3,1,2,0:T(8,128)}, f32[4,32,1,1024]{3,1,2,0:T(8,128)}, u32[]{:S(2)}, u32[]{:S(2)}) collective-permute-start(f32[4,32,1,1024]{3,1,2,0:T(8,128)} %get-tuple-element.16), channel_id=1, source_target_pairs={{1,0},{2,1},{3,2},{4,3},{5,4},{6,5},{7,6},{9,8},{10,9},{11,10},{12... | collective-permute-start | bytes 1572872 | tf_op jit(solution)/shard_map/ppermute | solution.py:18
  504.0 331.9 %collective-permute-start.7 = (f32[4,32,1,1024]{3,1,2,0:T(8,128)}, f32[4,32,1,1024]{3,1,2,0:T(8,128)}, u32[]{:S(2)}, u32[]{:S(2)}) collective-permute-start(f32[4,32,1,1024]{3,1,2,0:T(8,128)} %get-tuple-element.15), channel_id=1, source_target_pairs={{0,1},{1,2},{2,3},{3,4},{4,5},{5,6},{6,7},{8,9},{9,10},{10,11},{11... | collective-permute-start | bytes 1572872 | tf_op jit(solution)/shard_map/ppermute | solution.py:17
  553.6 5.1 copy-start.21
  564.1 5.4 copy-start.29
  564.1 264.4 %all-to-all-start.7 = ((f32[64,32,256]{2,1,0:T(8,128)}), f32[64,32,256]{2,1,0:T(8,128)}, u32[]{:S(2)}, u32[]{:S(2)}) async-start(f32[64,32,256]{2,1,0:T(8,128)} %bitcast.437), calls=%async_computation.7 | async-start | bytes 4194304 | tf_op jit(solution)/shard_map/all_to_all | solution.py:168
  569.5 214.2 %all-reduce.3.cloned.1.call-start = ((), (), s32[]{:S(2)}) async-start(), calls=%async_computation.8 | async-start | bytes 2097152
  (23 other events, 71.7 us)
Sparse Core Ops, SparseCore 0:
  666.7 117.0 all-reduce.2
where the time goes:
time: 862 us; the launch traced here: 852 us
  blocking collectives  230 us (27%)
  waiting for transfers between devices  194 us (23%)
  local copies, waits for them, and re-layouts  186 us (22%)
  matrix products  138 us (16%)
  starting transfers between devices  53.3 us (6%)
  other arithmetic  35.2 us (4%)
  between operations  15.6 us (2%)
    unnamed x2, waiting for transfers between devices  113 us
    unnamed x102, local copies, waits for them, and re-layouts  103 us
    psum x1, blocking collectives, on_device(): kernel_total = lax.psum(jnp.stack(kernel_pieces[::-1]), ('tm', 'space'))  88 us
    all_to_all x2, blocking collectives, on_device(): lax.all_to_all(flattened, 'tm', split_axis=2, concat_axis=0, tiled=True)  65.8 us
    ppermute x4, waiting for transfers between devices, extended(): before = lax.ppermute(last, axis, up)  46.8 us
    psum x1, blocking collectives, on_device(): mode_total = lax.psum(mode_stack, 'space')  43.4 us
    all_to_all x1, blocking collectives, on_device(): lax.all_to_all(flat_sens, 'tm', split_axis=2, concat_axis=0, tiled=True)  32.9 us
    ppermute x4, waiting for transfers between devices, extended(): after = lax.ppermute(initial, axis, down)  32.3 us
  transfers between devices with their start and end apart: 14, of which 7 were waited for; matrix products, arithmetic and copies ran while one was open for 15% of the time, Pallas kernels for 0%

commit v1 on v0

--- a/solution.py
+++ b/solution.py
@@ -1,3 +1,4 @@
+import functools
 import math
 import jax
 import jax.numpy as jnp
@@ -5,6 +6,18 @@
 from jax.sharding import PartitionSpec as P
 
 HIGHEST = lax.Precision.HIGHEST
+
+
+def return_all_area(my_data, peer_axis):
+    return jnp.concatenate(
+        lax.all_to_all(
+            jnp.stack(jnp.split(my_data, lax.axis_size(peer_axis), axis=2), 0), peer_axis, 0, 0
+        ),
+        0,
+    )
+
+
+refer_arrays = functools.partial(return_all_area, peer_axis="tm")
 
 
 def extended(value, sides, width):
@@ -160,7 +173,7 @@
         sens_padded = extended(sensitivity, (("space", 2),), 1)
         back_conv = convolve_adjoint(sens_padded, conv_kernel[layer_number], cells_x)
         flat_sens = sensitivity.reshape(time_local, channels, cell_count)
-        series_sens = lax.all_to_all(flat_sens, "tm", split_axis=2, concat_axis=0, tiled=True)
+        series_sens = refer_arrays(flat_sens)
         sens_modes = factor * forward_dft(cosine_all, sine_all, series_sens)
         mode_piece = weight_grad(coefficients, sens_modes)
         adjoint = channel_mix_adjoint(sens_modes, spectral_weights[layer_number])

time: 862 us -> 789 us (0.915)
  local copies, waits for them, and re-layouts: 186 us -> 134 us
  other arithmetic: 35.2 us -> 18 us
    unnamed x102 -> x124, local copies, waits for them, and re-layouts: 103 us -> 79.7 us
    all_to_all x2 -> x0, other arithmetic: 17.2 us -> none  [on_device(): lax.all_to_all(flat_sens, 'tm', split_axis=2, concat_axis=0, tiled=True)]
    all_to_all x2 -> x0, local copies, waits for them, and re-layouts: 16.5 us -> none  [on_device(): lax.all_to_all(flat_sens, 'tm', split_axis=2, concat_axis=0, tiled=True)]
    reshape x2, local copies, waits for them, and re-layouts: 13.8 us -> 0.37 us  [on_device(): flat_sens = sensitivity.reshape(time_local, channels, cell_count)]
  transfers between devices with their start and end apart: 14 -> 14, of which waited for: 7 -> 7; matrix products, arithmetic and copies ran while one was open for 15% -> 14% of each run, Pallas kernels for 0% -> 0%
where the time goes in v1:
time: 789 us; the launch traced here: 781 us
  blocking collectives  230 us (29%)
  waiting for transfers between devices  193 us (24%)
  matrix products  138 us (17%)
  local copies, waits for them, and re-layouts  134 us (17%)
  starting transfers between devices  53.3 us (7%)
  other arithmetic  18 us (2%)
  between operations  15.5 us (2%)
    unnamed x2, waiting for transfers between devices  113 us
    psum x1, blocking collectives, on_device(): kernel_total = lax.psum(jnp.stack(kernel_pieces[::-1]), ('tm', 'space'))  88 us
    unnamed x124, local copies, waits for them, and re-layouts  79.7 us
    all_to_all x2, blocking collectives, on_device(): lax.all_to_all(flattened, 'tm', split_axis=2, concat_axis=0, tiled=True)  65.8 us
    ppermute x4, waiting for transfers between devices, extended(): before = lax.ppermute(last, axis, up)  46.8 us
    psum x1, blocking collectives, on_device(): mode_total = lax.psum(mode_stack, 'space')  43.4 us
    all_to_all x1, blocking collectives, return_all_area(): lax.all_to_all(jnp.stack(jnp.split(my_data, lax.axis_size(peer_axis), axi...  32.4 us
    ppermute x4, waiting for transfers between devices, extended(): after = lax.ppermute(initial, axis, down)  31.3 us
  transfers between devices with their start and end apart: 14, of which 7 were waited for; matrix products, arithmetic and copies ran while one was open for 14% of the time, Pallas kernels for 0%

profile of v1, /device:TPU:0, one launch (start us, length us, event | category | flops | bytes accessed | tf_op | source)
XLA Modules:
  0.0 780.6 jit_solution(12259969831530154544)
XLA Ops:
  7.2 7.8 %copy.215 = f32[4,32,4,1024]{1,0,3,2:T(4,128)} copy(f32[4,32,4,1024]{3,2,1,0:T(4,128)} %param.5) | data formatting | bytes 4194304 | tf_op args[0]
  15.0 8.5 %reshape.151 = f32[16,1,32768]{2,1,0:T(1,128)S(1)} reshape(f32[4096,4,32]{2,1,0:T(4,128)} %bitcast.535) | data formatting | bytes 4194304
  23.5 33.1 %all_to_all.100 = f32[16,1,32768]{2,1,0:T(1,128)} all-to-all(f32[16,1,32768]{2,1,0:T(1,128)S(1)} %reshape.151), channel_id=1, replica_groups=mesh['tm'=16,'space'=8] {'tm'}, dimensions={0} | all-to-all | bytes 4194304 | tf_op jit(solution)/shard_map/all_to_all | solution.py:148
  57.1 7.3 reduce
  64.4 6.4 reshape.152
  70.8 6.8 copy.322
  108.7 23.0 %collective-permute-done = f32[4,32,1,1024]{3,1,2,0:T(8,128)S(1)} collective-permute-done((f32[4,32,1,1024]{3,1,2,0:T(8,128)S(1)}, f32[4,32,1,1024]{3,1,2,0:T(8,128)S(1)}, u32[]{:S(2)}, u32[]{:S(2)}) %collective-permute-start) | collective-permute-done | bytes 524320 | tf_op jit(solution)/shard_map/ppermute | solution.py:30
  134.7 11.6 %collective-permute-done.1 = f32[4,32,1,1024]{3,1,2,0:T(8,128)S(1)} collective-permute-done((f32[4,32,1,1024]{3,1,2,0:T(8,128)S(1)}, f32[4,32,1,1024]{3,1,2,0:T(8,128)S(1)}, u32[]{:S(2)}, u32[]{:S(2)}) %collective-permute-start.1) | collective-permute-done | bytes 524320 | tf_op jit(solution)/shard_map/ppermute | solution.py:31
  155.8 10.0 %multiply_multiply_fusion.10 = (f32[4,32,4,1024]{3,1,2,0:T(8,128)S(1)}, f32[4,32,4,1024]{3,1,2,0:T(8,128)}) fusion(f32[4,32,5,1024]{3,1,2,0:T(8,128)} %constant_dynamic-update-slice_fusion.2, f32[2,3,32,32]{3,2,1,0:T(8,128)S(1)} %copy-done.26, f32[32,4,4,1024]{3,0,2,1:T(8,128)} %fusion.186, f32[4,4,1024,32]{2,3,1,0:T(8,128)} %fusion.189, ...), kind=kOutput, calls=%fused_computation.86 | convolution fusion | flops 236453888 | bytes 13123584 | tf_op jit(solution)/shard_map/tcxs,cd->tdxs/dot_general | solution.py:107
  171.7 9.5 %reshape.153 = f32[16,1,32768]{2,1,0:T(1,128)} reshape(f32[4096,4,32]{2,1,0:T(4,128)} %bitcast.536) | data formatting | bytes 4194304
  181.2 32.7 %all_to_all.101 = f32[16,1,32768]{2,1,0:T(1,128)} all-to-all(f32[16,1,32768]{2,1,0:T(1,128)} %reshape.153), channel_id=1, replica_groups=mesh['tm'=16,'space'=8] {'tm'}, dimensions={0} | all-to-all | bytes 4194304 | tf_op jit(solution)/shard_map/all_to_all | solution.py:148
  213.9 8.6 %reduce.1 = f32[16,32768]{1,0:T(8,128)} reduce(f32[16,1,32768]{2,1,0:T(1,128)} %all_to_all.101, f32[]{:T(128)} %broadcast.353), dimensions={1}, to_apply=%all_to_all.78.reduce_sub_computation | reduce | bytes 4194308 | tf_op jit(solution)/shard_map/all_to_all | solution.py:148
  222.5 7.7 reshape.154
  230.2 8.2 %copy.235 = f32[4,32,16,256]{3,1,0,2:T(8,128)} copy(f32[4,32,16,256]{1,0,3,2:T(4,128)} %bitcast.534) | data formatting | bytes 4194304 | tf_op jit(solution)/shard_map/all_to_all | solution.py:148
  270.2 23.8 %collective-permute-done.2 = f32[4,32,1,1024]{3,1,2,0:T(8,128)S(1)} collective-permute-done((f32[4,32,1,1024]{3,1,2,0:T(8,128)S(1)}, f32[4,32,1,1024]{3,1,2,0:T(8,128)S(1)}, u32[]{:S(2)}, u32[]{:S(2)}) %collective-permute-start.2) | collective-permute-done | bytes 524320 | tf_op jit(solution)/shard_map/ppermute | solution.py:30
  309.0 9.8 %fusion.26 = f32[4,32,4,1024]{3,1,2,0:T(8,128)S(1)} fusion(f32[4,32,4,1024]{3,2,1,0:T(4,128)} %param.6, f32[4,4,1024,32]{2,3,1,0:T(8,128)} %fusion.20, f32[4,4,1024,32]{2,3,1,0:T(8,128)} %fusion.174, f32[4,32,4,1024]{3,2,1,0:T(4,128)} %reshape.120, f32[4,32,1,1024]{3,1,2,0:T(8,128)} %collective-permute-done.3, ...), kind=kOutput, calls=%fused_computation.38 | convolution fusion | flops 240779264 | bytes 13123584 | tf_op jit(solution)/shard_map/tcxs,cd->tdxs/dot_general | solution.py:107
  320.5 32.4 %all_to_all.102 = f32[16,4,32,256]{3,2,1,0:T(8,128)S(1)} all-to-all(f32[16,4,32,256]{3,2,1,0:T(8,128)S(1)} %fusion.148), channel_id=1, replica_groups=mesh['tm'=16,'space'=8] {'tm'}, dimensions={0} | all-to-all | bytes 4194304 | tf_op jit(solution)/shard_map/all_to_all | solution.py:13
  377.5 6.9 collective-permute-start.5
  395.3 16.3 %collective-permute-done.4 = f32[4,32,1,1024]{3,1,2,0:T(8,128)S(1)} collective-permute-done((f32[4,32,1,1024]{3,1,2,0:T(8,128)S(1)}, f32[4,32,1,1024]{3,1,2,0:T(8,128)S(1)}, u32[]{:S(2)}, u32[]{:S(2)}) %collective-permute-start.4) | collective-permute-done | bytes 524320 | tf_op jit(solution)/shard_map/ppermute | solution.py:31
  420.1 9.6 %multiply_add_fusion = f32[4,32,4,1024]{3,1,2,0:T(8,128)S(1)} fusion(f32[4,32,4,1024]{3,2,1,0:T(4,128)} %reshape.124, f32[4,4,1024,32]{2,3,1,0:T(8,128)} %fusion.2, f32[4,4,1024,32]{2,3,1,0:T(8,128)} %fusion.172, f32[4,32,4,1024]{3,1,2,0:T(8,128)} %get-tuple-element.30, f32[4,32,4,1024]{3,1,2,0:T(8,128)} %copy-done, ...), kind=kOutput, calls=%fused_computation.57 | convolution fusion | flops 240779264 | bytes 13123584 | tf_op jit(solution)/shard_map/tdxs,cd->tcxs/dot_general | solution.py:121
  455.6 7.2 collective-permute-start.7
  498.0 88.0 %psum.15 = f32[2,3,32,32]{3,2,1,0:T(8,128)} all-reduce(f32[2,3,32,32]{3,2,1,0:T(8,128)S(1)} %pad_maximum_fusion.11), channel_id=1, replica_groups=mesh['tm'=16,'space'=8] {'tm','space'}, use_global_device_ids=true, to_apply=%region_2.3 | all-reduce | flops 6144 | bytes 49152 | tf_op jit(solution)/shard_map/psum | solution.py:185
  599.5 112.7 %all-reduce.3.cloned.1.call-done = f32[2,2,16,32,32]{4,3,2,1,0:T(8,128)} async-done(((f32[2,2,16,32,32]{4,3,2,1,0:T(8,128)}), f32[2,2,16,32,32]{4,3,2,1,0:T(8,128)}) %all-reduce.3.cloned.1.call-update) | async-done | bytes 262160
  713.7 43.4 %psum.14 = f32[2,2,1,32,32]{4,3,2,1,0:T(8,128)} all-reduce(f32[2,2,1,32,32]{4,3,2,1,0:T(8,128)S(1)} %constant_dynamic-slice_fusion), channel_id=1, replica_groups=mesh['tm'=16,'space'=8] {'space'}, use_global_device_ids=true, to_apply=%region_1.2 | all-reduce | flops 4096 | bytes 32768 | tf_op jit(solution)/shard_map/psum | solution.py:189
  (226 shorter events, 233.6 us)
Async XLA Ops:
  92.6 58.0 %all-to-all-start.1 = ((f32[64,32,256]{2,1,0:T(8,128)}), f32[64,32,256]{2,1,0:T(8,128)}, u32[]{:S(2)}, u32[]{:S(2)}) async-start(f32[64,32,256]{2,1,0:T(8,128)} %bitcast.589), calls=%async_computation.1 | async-start | bytes 4194304 | tf_op jit(solution)/shard_map/all_to_all | solution.py:152
  97.2 7.2 copy-start.26
  98.1 33.6 %collective-permute-start = (f32[4,32,1,1024]{3,1,2,0:T(8,128)S(1)}, f32[4,32,1,1024]{3,1,2,0:T(8,128)S(1)}, u32[]{:S(2)}, u32[]{:S(2)}) collective-permute-start(f32[4,32,1,1024]{3,1,2,0:T(8,128)S(1)} %copy.453), channel_id=1, source_target_pairs={{0,1},{1,2},{2,3},{3,4},{4,5},{5,6},{6,7},{8,9},{9,10},{10,11},{11... | collective-permute-start | bytes 1572872 | tf_op jit(solution)/shard_map/ppermute | solution.py:30
  103.1 43.2 %collective-permute-start.1 = (f32[4,32,1,1024]{3,1,2,0:T(8,128)S(1)}, f32[4,32,1,1024]{3,1,2,0:T(8,128)S(1)}, u32[]{:S(2)}, u32[]{:S(2)}) collective-permute-start(f32[4,32,1,1024]{3,1,2,0:T(8,128)S(1)} %copy.454), channel_id=1, source_target_pairs={{1,0},{2,1},{3,2},{4,3},{5,4},{6,5},{7,6},{9,8},{10,9},{11,10},{12... | collective-permute-start | bytes 1572872 | tf_op jit(solution)/shard_map/ppermute | solution.py:31
  134.7 12.4 %copy-start.22 = (f32[4,32,5,1024]{3,1,2,0:T(8,128)}, f32[4,32,5,1024]{3,1,2,0:T(8,128)S(1)}, u32[]{:S(2)}) copy-start(f32[4,32,5,1024]{3,1,2,0:T(8,128)S(1)} %get-tuple-element.24) | copy-start | bytes 7864324
  255.1 43.2 %all-to-all-start.3 = ((f32[64,32,256]{2,1,0:T(8,128)}), f32[64,32,256]{2,1,0:T(8,128)}, u32[]{:S(2)}, u32[]{:S(2)}) async-start(f32[64,32,256]{2,1,0:T(8,128)} %bitcast.590), calls=%async_computation.3 | async-start | bytes 4194304 | tf_op jit(solution)/shard_map/all_to_all | solution.py:152
  260.4 33.6 %collective-permute-start.2 = (f32[4,32,1,1024]{3,1,2,0:T(8,128)S(1)}, f32[4,32,1,1024]{3,1,2,0:T(8,128)S(1)}, u32[]{:S(2)}, u32[]{:S(2)}) collective-permute-start(f32[4,32,1,1024]{3,1,2,0:T(8,128)S(1)} %get-tuple-element.20), channel_id=1, source_target_pairs={{0,1},{1,2},{2,3},{3,4},{4,5},{5,6},{6,7},{8,9},{9,10},{10,11},{11... | collective-permute-start | bytes 1572872 | tf_op jit(solution)/shard_map/ppermute | solution.py:30
  265.6 43.5 %collective-permute-start.3 = (f32[4,32,1,1024]{3,1,2,0:T(8,128)}, f32[4,32,1,1024]{3,1,2,0:T(8,128)}, u32[]{:S(2)}, u32[]{:S(2)}) collective-permute-start(f32[4,32,1,1024]{3,1,2,0:T(8,128)} %get-tuple-element.19), channel_id=1, source_target_pairs={{1,0},{2,1},{3,2},{4,3},{5,4},{6,5},{7,6},{9,8},{10,9},{11,10},{12... | collective-permute-start | bytes 1572872 | tf_op jit(solution)/shard_map/ppermute | solution.py:31
  368.9 46.2 %all-to-all-start.5 = ((f32[64,32,256]{2,1,0:T(8,128)}), f32[64,32,256]{2,1,0:T(8,128)}, u32[]{:S(2)}, u32[]{:S(2)}) async-start(f32[64,32,256]{2,1,0:T(8,128)} %bitcast.588), calls=%async_computation.5 | async-start | bytes 4194304 | tf_op jit(solution)/shard_map/all_to_all | solution.py:181
  373.5 10.9 %copy-start.1 = (f32[4,32,4,1024]{3,1,2,0:T(8,128)S(1)}, f32[4,32,4,1024]{3,1,2,0:T(8,128)}, u32[]{:S(2)}) copy-start(f32[4,32,4,1024]{3,1,2,0:T(8,128)} %copy-done) | copy-start | bytes 6291460
  376.2 35.4 %collective-permute-start.4 = (f32[4,32,1,1024]{3,1,2,0:T(8,128)S(1)}, f32[4,32,1,1024]{3,1,2,0:T(8,128)S(1)}, u32[]{:S(2)}, u32[]{:S(2)}) collective-permute-start(f32[4,32,1,1024]{3,1,2,0:T(8,128)S(1)} %get-tuple-element.18), channel_id=1, source_target_pairs={{1,0},{2,1},{3,2},{4,3},{5,4},{6,5},{7,6},{9,8},{10,9},{11,10},{12... | collective-permute-start | bytes 1572872 | tf_op jit(solution)/shard_map/ppermute | solution.py:31
  377.5 42.7 %collective-permute-start.5 = (f32[4,32,1,1024]{3,1,2,0:T(8,128)}, f32[4,32,1,1024]{3,1,2,0:T(8,128)}, u32[]{:S(2)}, u32[]{:S(2)}) collective-permute-start(f32[4,32,1,1024]{3,1,2,0:T(8,128)} %get-tuple-element.17), channel_id=1, source_target_pairs={{0,1},{1,2},{2,3},{3,4},{4,5},{5,6},{6,7},{8,9},{9,10},{10,11},{11... | collective-permute-start | bytes 1572872 | tf_op jit(solution)/shard_map/ppermute | solution.py:30
  440.6 33.0 %all-to-all-start.6 = ((f32[16,4,32,256]{3,2,1,0:T(8,128)}), f32[16,4,32,256]{3,2,1,0:T(8,128)}, u32[]{:S(2)}, u32[]{:S(2)}) async-start(f32[16,4,32,256]{3,2,1,0:T(8,128)} %fusion.132), calls=%async_computation.6 | async-start | bytes 4194304 | tf_op jit(solution)/shard_map/all_to_all | solution.py:13
  445.8 4.6 copy-start.13
  445.8 4.6 copy-start.17
  445.8 5.8 copy-start.9
  445.8 5.8 copy-start.15
  451.7 11.2 %copy-start.3 = (f32[4,32,4,1024]{3,2,1,0:T(4,128)S(1)}, f32[4,32,4,1024]{3,2,1,0:T(4,128)}, u32[]{:S(2)}) copy-start(f32[4,32,4,1024]{3,2,1,0:T(4,128)} %param.5) | copy-start | bytes 6291460
  454.3 140.7 %collective-permute-start.6 = (f32[4,32,1,1024]{3,1,2,0:T(8,128)}, f32[4,32,1,1024]{3,1,2,0:T(8,128)}, u32[]{:S(2)}, u32[]{:S(2)}) collective-permute-start(f32[4,32,1,1024]{3,1,2,0:T(8,128)} %get-tuple-element.16), channel_id=1, source_target_pairs={{1,0},{2,1},{3,2},{4,3},{5,4},{6,5},{7,6},{9,8},{10,9},{11,10},{12... | collective-permute-start | bytes 1572872 | tf_op jit(solution)/shard_map/ppermute | solution.py:31
  455.6 308.8 %collective-permute-start.7 = (f32[4,32,1,1024]{3,1,2,0:T(8,128)}, f32[4,32,1,1024]{3,1,2,0:T(8,128)}, u32[]{:S(2)}, u32[]{:S(2)}) collective-permute-start(f32[4,32,1,1024]{3,1,2,0:T(8,128)} %get-tuple-element.15), channel_id=1, source_target_pairs={{0,1},{1,2},{2,3},{3,4},{4,5},{5,6},{6,7},{8,9},{9,10},{10,11},{11... | collective-permute-start | bytes 1572872 | tf_op jit(solution)/shard_map/ppermute | solution.py:30
  492.6 5.4 copy-start.27
  492.6 264.5 %all-to-all-start.7 = ((f32[64,32,256]{2,1,0:T(8,128)}), f32[64,32,256]{2,1,0:T(8,128)}, u32[]{:S(2)}, u32[]{:S(2)}) async-start(f32[64,32,256]{2,1,0:T(8,128)} %bitcast.587), calls=%async_computation.7 | async-start | bytes 4194304 | tf_op jit(solution)/shard_map/all_to_all | solution.py:181
  497.9 214.3 %all-reduce.3.cloned.1.call-start = ((), (), s32[]{:S(2)}) async-start(), calls=%async_computation.8 | async-start | bytes 2097152
  586.0 4.7 copy-start.21
  (21 other events, 59.5 us)
Sparse Core Ops, SparseCore 0:
  595.1 117.0 all-reduce.2
